TPU v7x, 256 devices: a whole 4x4x8 slice. The times are simulated.
256 devices in a mesh: row: 16 (over z, core), col: 16 (over x, y).
Axes of the slice: x: 4, y: 4, z: 8, core: 2. Of those that a mesh axis runs over, the one named last changes fastest.
Arguments:
- inputs: bfloat16 [4096, 18432], P('col', 'row'), may hold values from -6 to 6
- out_grads: bfloat16 [4096, 18432], P('row', 'col'), may hold values from -0.09375 to 0.09375
- range_test: float32 [18432, 128], P('col'), may hold values from -0.046875 to 0.046875
- corange_test: float32 [256, 18432], P(None, 'row'), may hold values from -0.046875 to 0.046875
Outputs:
- range_sketch: float32 [18432, 128], P('row')
- corange_sketch: float32 [256, 18432], P(None, 'col')
- residual: float32 [18432, 18432], P('row', 'col')
All inputs are finite; a program needn't handle non-finite values.
Results may differ from a plain program's by a relative error of at most 0.0003.
Values may be sent and summed in bfloat16 or wider, within the bound.
A program may use at most 128 MiB of HBM per device.

v0:
```python
import jax
import jax.numpy as jnp
from jax import lax
from jax.sharding import PartitionSpec as P

highest = lax.Precision.HIGHEST


def token_product(left_rows, right_rows):
    return lax.dot_general(
        left_rows, right_rows, (((0,), (0,)), ((), ())), preferred_element_type=jnp.float32
    )


def exact_product(left_side, right_side):
    return jnp.dot(left_side, right_side, precision=highest, preferred_element_type=jnp.float32)


def per_device(inputs, out_grads, range_test, corange_test):
    grads_all = lax.all_gather(out_grads, "row", axis=0, tiled=True)
    gradient = token_product(lax.all_gather(inputs, "col", axis=0, tiled=True), grads_all)
    range_sketch = lax.psum(exact_product(gradient, range_test), "col")
    corange_sketch = lax.psum(exact_product(corange_test, gradient), "row")
    core_input = lax.psum(exact_product(corange_test, range_sketch), "row")
    gram_matrix = lax.dot_general(
        core_input,
        core_input,
        (((0,), (0,)), ((), ())),
        precision=highest,
        preferred_element_type=jnp.float32,
    )
    factor_low = jnp.linalg.cholesky(gram_matrix)
    core_map = jax.scipy.linalg.cho_solve((factor_low, True), core_input.T)
    project = exact_product(core_map, corange_sketch)
    residual = gradient - exact_product(range_sketch, project)
    return (range_sketch, corange_sketch, residual)


def solution(mesh):
    placed = (P("col", "row"), P("row", "col"), P("col", None), P(None, "row"))
    return jax.shard_map(
        per_device,
        mesh=mesh,
        in_specs=placed,
        out_specs=(P("row", None), P(None, "col"), P("row", "col")),
        check_vma=False,
    )
```

profile of v0, /device:TPU:1, one launch (start us, length us, event | category | flops | bytes accessed | tf_op | source)
XLA Modules:
  0.0 438.1 jit_solution(6629856623916740087)
XLA Ops:
  7.2 0.0 copy-start
  7.2 0.0 all-gather.3.cloned.1.call-start
  7.2 0.7 all-gather.3.cloned.1.call-update
  7.9 0.0 all-gather.5.cloned.1.call-start
  8.0 0.7 all-gather.5.cloned.1.call-update
  8.7 0.0 copy-start.3
  8.7 0.0 all-reduce.4.cloned.1.call-start
  8.7 86.0 %all-gather.3.cloned.1.call-done = bf16[4096,1152]{1,0:T(8,128)(2,1)} async-done(((bf16[256,1152]{1,0:T(8,128)(2,1)}), bf16[4096,1152]{1,0:T(8,128)(2,1)}) %all-gather.3.cloned.1.call-update) | async-done | bytes 9437200 | tf_op jit(solution)/shard_map/all_gather | solution.py:21
  94.7 63.0 %all-gather.5.cloned.1.call-done = bf16[4096,1152]{1,0:T(8,128)(2,1)} async-done(((bf16[256,1152]{1,0:T(8,128)(2,1)}), bf16[4096,1152]{1,0:T(8,128)(2,1)}) %all-gather.5.cloned.1.call-update) | async-done | bytes 9437200 | tf_op jit(solution)/shard_map/all_gather | solution.py:20
  157.6 17.0 %fusion.6 = f32[1152,1152]{1,0:T(8,128)S(1)} fusion(bf16[4096,1152]{1,0:T(8,128)(2,1)} %all-gather.3.cloned.1.call-done, bf16[4096,1152]{1,0:T(8,128)(2,1)} %all-gather.5.cloned.1.call-done), kind=kOutput, calls=%fused_computation.15 | convolution fusion | flops 10871635968 | bytes 24182784 | tf_op jit(solution)/shard_map/dot_general | solution.py:10
  174.7 0.0 copy-start.1
  174.7 2.4 copy-done.1
  177.1 0.0 copy-done.3
  177.1 5.3 %fusion.7 = f32[1152,128]{1,0:T(8,128)} fusion(f32[1152,1152]{1,0:T(8,128)S(1)} %fusion.6, f32[1152,128]{1,0:T(8,128)S(1)} %copy-done.3), kind=kOutput, calls=%fused_computation.16 | convolution fusion | flops 2038431744 | bytes 6488064 | tf_op jit(solution)/shard_map/dot_general | solution.py:16
  182.4 0.0 all-reduce.4.cloned.1.call-update
  182.4 0.2 all-reduce.6.cloned.1.call-start
  182.6 0.0 copy-done
  182.7 12.0 %convolution_bitcast_fusion = f32[256,1152]{0,1:T(8,128)} fusion(f32[1152,1152]{1,0:T(8,128)} %copy-done.1, f32[256,1152]{1,0:T(8,128)S(1)} %copy-done), kind=kOutput, calls=%fused_computation.1 | convolution fusion | flops 4076863488 | bytes 7667712 | tf_op jit(solution)/shard_map/dot_general | solution.py:16
  194.6 79.5 %all-reduce.4.cloned.1.call-done = f32[1152,128]{1,0:T(8,128)} async-done(((f32[1152,128]{1,0:T(8,128)}), f32[1152,128]{1,0:T(8,128)}) %all-reduce.4.cloned.1.call-update) | async-done | bytes 589840 | tf_op jit(solution)/shard_map/psum | solution.py:22
  274.1 0.0 copy-start.2
  274.1 3.0 convolution_bitcast_fusion.1
  277.1 0.0 all-reduce.6.cloned.1.call-update
  277.1 114.8 %all-reduce.6.cloned.1.call-done = (f32[256,1152]{0,1:T(8,128)}, f32[256,128]{0,1:T(8,128)}) async-done(((f32[256,1152]{0,1:T(8,128)}, f32[256,128]{0,1:T(8,128)}), (f32[256,1152]{0,1:T(8,128)}, f32[256,128]{0,1:T(8,128)})) %all-reduce.6.cloned.1.call-update) | async-done | bytes 1310736 | tf_op jit(solution)/shard_map/psum | solution.py:23
  392.0 1.3 fusion.8
  393.2 0.1 copy.7
  393.3 11.9 %cholesky.16 = f32[128,128]{1,0:T(8,128)S(1)} custom-call(f32[128,128]{1,0:T(8,128)S(1)} %fusion.5), custom_call_target="Cholesky" | custom-call | tf_op jit(solution)/shard_map/jit(cholesky)/cholesky | solution.py:32
  405.3 0.6 compare_reduce_fusion
  405.9 0.7 fusion
  406.6 9.8 %custom-call.10 = f32[1,128,128]{1,2,0:T(8,128)S(1)} custom-call(f32[1,128,128]{2,1,0:T(8,128)S(1)} %fusion), custom_call_target="InvertDiagBlocksLowerTriangular" | custom-call | tf_op jit(solution)/shard_map/jit(_cho_solve)/triangular_solve | solution.py:33
  416.4 1.2 fusion.3
  417.6 0.3 fusion.1
  417.9 2.7 copy.8
  420.6 2.5 fusion.9
  423.0 0.0 copy-done.2
  423.1 7.7 %convolution_subtract_fusion = f32[1152,1152]{1,0:T(8,128)} fusion(f32[1152,1152]{1,0:T(8,128)} %copy-done.1, f32[1152,128]{1,0:T(8,128)S(1)} %copy-done.2, f32[128,1152]{1,0:T(8,128)S(1)} %fusion.9), kind=kOutput, calls=%fused_computation | convolution fusion | flops 2039758848 | bytes 11796480 | tf_op jit(solution)/shard_map/dot_general | solution.py:16
  430.8 0.8 copy.12
  (2 shorter events, 0.0 us)
Async XLA Ops:
  7.2 175.5 %copy-start = (f32[256,1152]{1,0:T(8,128)S(1)}, f32[256,1152]{1,0:T(8,128)}, u32[]{:S(2)}) copy-start(f32[256,1152]{1,0:T(8,128)} %param.7) | copy-start | bytes 3538948
  7.2 87.5 %all-gather.3.cloned.1.call-start = ((), (), s32[]{:S(2)}) async-start(), calls=%async_computation | async-start | bytes 10027008 | tf_op jit(solution)/shard_map/all_gather | solution.py:21
  7.9 149.7 %all-gather.5.cloned.1.call-start = ((), (), s32[]{:S(2)}) async-start(), calls=%async_computation.1 | async-start | bytes 10027008 | tf_op jit(solution)/shard_map/all_gather | solution.py:20
  8.7 168.4 %copy-start.3 = (f32[1152,128]{1,0:T(8,128)S(1)}, f32[1152,128]{1,0:T(8,128)}, u32[]{:S(2)}) copy-start(f32[1152,128]{1,0:T(8,128)} %param.6) | copy-start | bytes 1769476
  8.7 265.4 %all-reduce.4.cloned.1.call-start = ((), (), s32[]{:S(2)}) async-start(), calls=%async_computation.2 | async-start | bytes 1179648 | tf_op jit(solution)/shard_map/psum | solution.py:22
  174.7 2.4 copy-start.1
  182.4 209.6 %all-reduce.6.cloned.1.call-start = ((), (), s32[]{:S(2)}) async-start(), calls=%async_computation.3 | async-start | bytes 2621440 | tf_op jit(solution)/shard_map/psum | solution.py:23
  274.1 149.0 %copy-start.2 = (f32[1152,128]{1,0:T(8,128)S(1)}, f32[1152,128]{1,0:T(8,128)}, u32[]{:S(2)}) copy-start(f32[1152,128]{1,0:T(8,128)} %all-reduce.4.cloned.1.call-done) | copy-start | bytes 1769476
Sparse Core Ops, SparseCore 0:
  10.5 84.1 all-gather.2
  96.5 61.0 all-gather.4
  182.5 91.4 all-reduce.3
  277.3 114.6 all-reduce.5
where the time goes:
time: 438 us
  waiting for transfers between devices  345 us (79%)
  matrix products  50.3 us (11%)
  other arithmetic  23.1 us (5%)
  between operations  13.9 us (3%)
  local copies, waits for them, and re-layouts  5.95 us (1%)
    psum x1, waiting for transfers between devices, per_device(): corange_sketch = lax.psum(exact_product(corange_test, gradient), 'row')  115 us
    all_gather x1, waiting for transfers between devices, per_device(): lax.all_gather(inputs, 'col', axis=0, tiled=True)  86 us
    psum x1, waiting for transfers between devices, per_device(): range_sketch = lax.psum(exact_product(gradient, range_test), 'col')  79.5 us
    all_gather x1, waiting for transfers between devices, per_device(): grads_all = lax.all_gather(out_grads, 'row', axis=0, tiled=True)  63 us
    dot_general x5, matrix products, exact_product(): jnp.dot(left_side, right_side, precision=highest, preferred_element_type=...  30.5 us
    dot_general x1, matrix products, token_product(): lax.dot_general(left_rows, right_rows, (((0,), (0,)), ((), ())), preferre...  17 us
    another operation x3, other arithmetic, per_device(): factor_low = jnp.linalg.cholesky(gram_matrix)  12.6 us
    another operation x2, other arithmetic, per_device(): core_map = jax.scipy.linalg.cho_solve((factor_low, True), core_input.T)  10.5 us
  transfers between devices with their start and end apart: 4, of which 4 were waited for; matrix products, arithmetic and copies ran while one was open for 3% of the time, Pallas kernels for 0%

commit v1 on v0

--- a/solution.py
+++ b/solution.py
@@ -17,7 +17,9 @@
 
 
 def per_device(inputs, out_grads, range_test, corange_test):
-    grads_all = lax.all_gather(out_grads, "row", axis=0, tiled=True)
+    grads_all = jnp.concatenate(
+        lax.all_to_all(jnp.stack([out_grads] * lax.axis_size("row")), "row", 0, 0), axis=0
+    )
     gradient = token_product(lax.all_gather(inputs, "col", axis=0, tiled=True), grads_all)
     range_sketch = lax.psum(exact_product(gradient, range_test), "col")
     corange_sketch = lax.psum(exact_product(corange_test, gradient), "row")

time: 438 us -> 511 us (1.17)
  waiting for transfers between devices: 345 us -> 401 us
  starting transfers between devices: 0.34 us -> 10.3 us
  local copies, waits for them, and re-layouts: 5.95 us -> 12.1 us
    all_to_all x0 -> x1, waiting for transfers between devices: none -> 205 us  [per_device(): lax.all_to_all(jnp.stack([out_grads] * lax.axis_size('row')), 'row', 0, 0)]
    all_gather x1, waiting for transfers between devices: 86 us -> 0.01 us  [per_device(): lax.all_gather(inputs, 'col', axis=0, tiled=True)]
    all_gather x1 -> x0, waiting for transfers between devices: 63 us -> none  [per_device(): grads_all = lax.all_gather(out_grads, 'row', axis=0, tiled=True)]
    all_to_all x0 -> x1, starting transfers between devices: none -> 9.97 us  [per_device(): lax.all_to_all(jnp.stack([out_grads] * lax.axis_size('row')), 'row', 0, 0)]
    another operation x0 -> x1, local copies, waits for them, and re-layouts: none -> 6.15 us  [per_device(): jnp.stack([out_grads] * lax.axis_size('row'))]
  transfers between devices with their start and end apart: 4 -> 4, of which waited for: 4 -> 3; matrix products, arithmetic and copies ran while one was open for 3% -> 2% of each run, Pallas kernels for 0% -> 0%
where the time goes in v1:
time: 511 us
  waiting for transfers between devices  401 us (78%)
  matrix products  50.3 us (10%)
  other arithmetic  23.1 us (5%)
  between operations  13.9 us (3%)
  local copies, waits for them, and re-layouts  12.1 us (2%)
  starting transfers between devices  10.3 us (2%)
    all_to_all x1, waiting for transfers between devices, per_device(): lax.all_to_all(jnp.stack([out_grads] * lax.axis_size('row')), 'row', 0, 0)  205 us
    psum x1, waiting for transfers between devices, per_device(): corange_sketch = lax.psum(exact_product(corange_test, gradient), 'row')  115 us
    psum x1, waiting for transfers between devices, per_device(): range_sketch = lax.psum(exact_product(gradient, range_test), 'col')  80.8 us
    dot_general x5, matrix products, exact_product(): jnp.dot(left_side, right_side, precision=highest, preferred_element_type=...  30.5 us
    dot_general x1, matrix products, token_product(): lax.dot_general(left_rows, right_rows, (((0,), (0,)), ((), ())), preferre...  17.1 us
    another operation x3, other arithmetic, per_device(): factor_low = jnp.linalg.cholesky(gram_matrix)  12.6 us
    another operation x2, other arithmetic, per_device(): core_map = jax.scipy.linalg.cho_solve((factor_low, True), core_input.T)  10.5 us
  transfers between devices with their start and end apart: 4, of which 3 were waited for; matrix products, arithmetic and copies ran while one was open for 2% of the time, Pallas kernels for 0%

profile of v1, /device:TPU:1, one launch (start us, length us, event | category | flops | bytes accessed | tf_op | source)
XLA Modules:
  0.0 511.0 jit_solution(9506117028227731135)
XLA Ops:
  7.2 0.0 copy-start
  7.2 6.1 %stack.2 = bf16[16,256,1152]{2,1,0:T(8,128)(2,1)} broadcast(bf16[256,1152]{1,0:T(8,128)(2,1)} %param.5), dimensions={1,2} | broadcast | bytes 10027008 | tf_op jit(solution)/shard_map/stack | solution.py:21
  13.3 10.0 %all-to-all-start = ((bf16[16,256,1152]{2,1,0:T(8,128)(2,1)}), bf16[16,256,1152]{2,1,0:T(8,128)(2,1)}, u32[]{:S(2)}, u32[]{:S(2)}) async-start(bf16[16,256,1152]{2,1,0:T(8,128)(2,1)} %stack.2), calls=%async_computation | async-start | bytes 18874368 | tf_op jit(solution)/shard_map/all_to_all | solution.py:21
  23.3 0.0 all-gather.2.cloned.1.call-start
  23.3 0.7 all-gather.2.cloned.1.call-update
  24.0 0.0 all-reduce.4.cloned.1.call-start
  24.1 205.0 %all-to-all-done = bf16[16,256,1152]{2,1,0:T(8,128)(2,1)} async-done(((bf16[16,256,1152]{2,1,0:T(8,128)(2,1)}), bf16[16,256,1152]{2,1,0:T(8,128)(2,1)}, u32[]{:S(2)}, u32[]{:S(2)}) %all-to-all-start) | async-done | bytes 9437216 | tf_op jit(solution)/shard_map/all_to_all | solution.py:21
  229.1 0.0 all-gather.2.cloned.1.call-done
  229.1 0.0 copy-start.3
  229.1 17.1 %fusion.6 = f32[1152,1152]{1,0:T(8,128)S(1)} fusion(bf16[4096,1152]{1,0:T(8,128)(2,1)} %all-gather.2.cloned.1.call-done, bf16[4096,1152]{1,0:T(8,128)(2,1)} %bitcast), kind=kOutput, calls=%fused_computation.15 | convolution fusion | flops 10871635968 | bytes 24182784 | tf_op jit(solution)/shard_map/dot_general | solution.py:10
  246.2 0.0 copy-start.1
  246.2 2.4 copy-done.1
  248.6 0.0 copy-done.3
  248.6 5.3 %fusion.7 = f32[1152,128]{1,0:T(8,128)} fusion(f32[1152,1152]{1,0:T(8,128)S(1)} %fusion.6, f32[1152,128]{1,0:T(8,128)S(1)} %copy-done.3), kind=kOutput, calls=%fused_computation.16 | convolution fusion | flops 2038431744 | bytes 6488064 | tf_op jit(solution)/shard_map/dot_general | solution.py:16
  253.9 0.0 all-reduce.4.cloned.1.call-update
  253.9 0.2 all-reduce.6.cloned.1.call-start
  254.2 0.0 copy-done
  254.2 12.0 %convolution_bitcast_fusion = f32[256,1152]{0,1:T(8,128)} fusion(f32[1152,1152]{1,0:T(8,128)} %copy-done.1, f32[256,1152]{1,0:T(8,128)S(1)} %copy-done), kind=kOutput, calls=%fused_computation.1 | convolution fusion | flops 4076863488 | bytes 7667712 | tf_op jit(solution)/shard_map/dot_general | solution.py:16
  266.1 80.8 %all-reduce.4.cloned.1.call-done = f32[1152,128]{1,0:T(8,128)} async-done(((f32[1152,128]{1,0:T(8,128)}), f32[1152,128]{1,0:T(8,128)}) %all-reduce.4.cloned.1.call-update) | async-done | bytes 589840 | tf_op jit(solution)/shard_map/psum | solution.py:24
  347.0 0.0 copy-start.2
  347.0 3.0 convolution_bitcast_fusion.1
  350.0 0.0 all-reduce.6.cloned.1.call-update
  350.0 114.8 %all-reduce.6.cloned.1.call-done = (f32[256,1152]{0,1:T(8,128)}, f32[256,128]{0,1:T(8,128)}) async-done(((f32[256,1152]{0,1:T(8,128)}, f32[256,128]{0,1:T(8,128)}), (f32[256,1152]{0,1:T(8,128)}, f32[256,128]{0,1:T(8,128)})) %all-reduce.6.cloned.1.call-update) | async-done | bytes 1310736 | tf_op jit(solution)/shard_map/psum | solution.py:25
  464.9 1.3 fusion.8
  466.1 0.1 copy.7
  466.3 11.9 %cholesky.16 = f32[128,128]{1,0:T(8,128)S(1)} custom-call(f32[128,128]{1,0:T(8,128)S(1)} %fusion.5), custom_call_target="Cholesky" | custom-call | tf_op jit(solution)/shard_map/jit(cholesky)/cholesky | solution.py:34
  478.2 0.6 compare_reduce_fusion
  478.9 0.7 fusion
  479.5 9.8 %custom-call.10 = f32[1,128,128]{1,2,0:T(8,128)S(1)} custom-call(f32[1,128,128]{2,1,0:T(8,128)S(1)} %fusion), custom_call_target="InvertDiagBlocksLowerTriangular" | custom-call | tf_op jit(solution)/shard_map/jit(_cho_solve)/triangular_solve | solution.py:35
  489.3 1.2 fusion.3
  490.6 0.3 fusion.1
  490.8 2.7 copy.8
  493.5 2.5 fusion.9
  496.0 0.0 copy-done.2
  496.0 7.7 %convolution_subtract_fusion = f32[1152,1152]{1,0:T(8,128)} fusion(f32[1152,1152]{1,0:T(8,128)} %copy-done.1, f32[1152,128]{1,0:T(8,128)S(1)} %copy-done.2, f32[128,1152]{1,0:T(8,128)S(1)} %fusion.9), kind=kOutput, calls=%fused_computation | convolution fusion | flops 2039758848 | bytes 11796480 | tf_op jit(solution)/shard_map/dot_general | solution.py:16
  503.7 0.8 copy.12
  (2 shorter events, 0.0 us)
Async XLA Ops:
  7.2 247.0 %copy-start = (f32[256,1152]{1,0:T(8,128)S(1)}, f32[256,1152]{1,0:T(8,128)}, u32[]{:S(2)}) copy-start(f32[256,1152]{1,0:T(8,128)} %param.7) | copy-start | bytes 3538948
  13.3 215.8 %all-to-all-start = ((bf16[16,256,1152]{2,1,0:T(8,128)(2,1)}), bf16[16,256,1152]{2,1,0:T(8,128)(2,1)}, u32[]{:S(2)}, u32[]{:S(2)}) async-start(bf16[16,256,1152]{2,1,0:T(8,128)(2,1)} %stack.2), calls=%async_computation | async-start | bytes 18874368 | tf_op jit(solution)/shard_map/all_to_all | solution.py:21
  23.3 205.8 %all-gather.2.cloned.1.call-start = ((), (), s32[]{:S(2)}) async-start(), calls=%async_computation.1 | async-start | bytes 10027008 | tf_op jit(solution)/shard_map/all_gather | solution.py:23
  24.0 322.9 %all-reduce.4.cloned.1.call-start = ((), (), s32[]{:S(2)}) async-start(), calls=%async_computation.2 | async-start | bytes 1179648 | tf_op jit(solution)/shard_map/psum | solution.py:24
  229.1 19.5 %copy-start.3 = (f32[1152,128]{1,0:T(8,128)S(1)}, f32[1152,128]{1,0:T(8,128)}, u32[]{:S(2)}) copy-start(f32[1152,128]{1,0:T(8,128)} %param.6) | copy-start | bytes 1769476
  246.2 2.4 copy-start.1
  253.9 210.9 %all-reduce.6.cloned.1.call-start = ((), (), s32[]{:S(2)}) async-start(), calls=%async_computation.3 | async-start | bytes 2621440 | tf_op jit(solution)/shard_map/psum | solution.py:25
  347.0 149.0 %copy-start.2 = (f32[1152,128]{1,0:T(8,128)S(1)}, f32[1152,128]{1,0:T(8,128)}, u32[]{:S(2)}) copy-start(f32[1152,128]{1,0:T(8,128)} %all-reduce.4.cloned.1.call-done) | copy-start | bytes 1769476
Sparse Core Ops, SparseCore 0:
  26.6 81.4 all-gather.1
  254.1 92.8 all-reduce.3
  350.2 114.6 all-reduce.5
